TPU v7x, 512 devices: a whole 4x4x16 slice. The times are simulated.
512 devices in a mesh: gx: 32 (over z_hi, y, x), gz: 16 (over z_lo, core).
Axes of the slice: x: 4, y: 4, z: 16 (z_hi: 2, z_lo: 8; z = z_hi * 8 + z_lo), core: 2. Of those that a mesh axis runs over, the one named last changes fastest.
Arguments:
- field: bfloat16 [2048, 16, 2048], P('gx', None, 'gz'), may hold values from -6 to 6
- even_vectors: bfloat16 [1024, 1024], P('gx', 'gz'), may hold values from -0.1875 to 0.1875
- odd_vectors: bfloat16 [1024, 1024], P('gx', 'gz'), may hold values from -0.1875 to 0.1875
Outputs:
- even_modes: float32 [1024, 16, 2048], P('gx', None, 'gz')
- odd_modes: float32 [1024, 16, 2048], P('gx', None, 'gz')
All inputs are finite; a program needn't handle non-finite values.
Results may differ from a plain program's by a relative error of at most 0.0031.
Values may be sent and summed in bfloat16 or wider, within the bound.
A program may use at most 64 MiB of HBM per device.

v0:
```python
import jax
import jax.numpy as jnp
from jax import lax
from jax.sharding import PartitionSpec as P


def rows_first(arrays, axis, dims):
    turned = [jnp.moveaxis(a, dim, 0) for a, dim in zip(arrays, dims)]
    widths = [t[0].size for t in turned]
    both = jnp.concatenate([t.reshape(-1, w) for t, w in zip(turned, widths)], axis=1)
    whole = lax.all_gather(both, axis, axis=0, tiled=True)
    parts = jnp.split(whole, [sum(widths[:k]) for k in range(1, len(widths))], axis=1)
    return tuple(
        (
            jnp.moveaxis(b.reshape(-1, *t.shape[1:]), 0, dim)
            for b, t, dim in zip(parts, turned, dims)
        )
    )


def local(field, even_vectors, odd_vectors):
    count = lax.axis_size("gx")
    width = field.shape[0]
    half_rows = width // 2
    planes = field.shape[1]
    depth = field.shape[2]
    order = count * half_rows
    even_block, odd_block = rows_first((even_vectors, odd_vectors), "gz", (1, 1))
    flat = field.reshape(width, planes * depth)
    lines = lax.all_to_all(flat, "gx", split_axis=1, concat_axis=0, tiled=True)
    lower = lines[:order].astype(jnp.float32)
    upper = lines[order:][::-1].astype(jnp.float32)
    both_parts = jnp.stack(
        ((lower + upper).astype(jnp.bfloat16), (lower - upper).astype(jnp.bfloat16))
    )
    stacked = jnp.stack((even_block, odd_block))
    all_modes = jnp.einsum(
        "prj,pjc->prc",
        lax.all_gather(stacked, "gx", axis=1, tiled=True),
        both_parts,
        preferred_element_type=jnp.float32,
    )
    returned = lax.all_to_all(all_modes, "gx", split_axis=1, concat_axis=2, tiled=True)
    even_modes = returned[0]
    odd_modes = returned[1]
    return (
        even_modes.reshape(even_block.shape[0], planes, depth),
        odd_modes.reshape(odd_block.shape[0], planes, depth),
    )


def solution(mesh):
    placed = (P("gx", None, "gz"), P("gx", "gz"), P("gx", "gz"))
    return jax.shard_map(
        local,
        mesh=mesh,
        in_specs=placed,
        out_specs=(P("gx", None, "gz"), P("gx", None, "gz")),
        check_vma=False,
    )
```

profile of v0, /device:TPU:96, one launch (start us, length us, event | category | flops | bytes accessed | tf_op | source)
XLA Modules:
  0.0 267.4 jit_solution(4487728167006009072)
XLA Ops:
  7.2 0.0 all-gather.2.cloned.1.call-start
  7.2 0.8 copy.14
  8.0 0.8 copy.15
  8.8 0.1 pad_maximum_fusion.1
  8.9 22.6 %all_gather.6 = bf16[1024,64]{1,0:T(8,128)(2,1)S(1)} all-gather(bf16[64,64]{1,0:T(8,128)(2,1)S(1)} %pad_maximum_fusion.1), channel_id=1, replica_groups=mesh['gx'=32,'gz'=16] {'gz'}, dimensions={0}, use_global_device_ids=true | all-gather | bytes 139264 | tf_op jit(solution)/shard_map/all_gather | solution.py:11
  31.5 0.1 fusion.11
  31.7 0.1 copy.25
  31.8 0.1 copy.26
  31.9 0.7 pad_maximum_fusion
  32.6 0.0 all-gather.2.cloned.1.call-update
  32.6 1.3 copy.18
  33.9 0.4 reshape.18
  34.3 35.5 %all_to_all.31 = bf16[32,2,2048]{2,1,0:T(2,128)(2,1)S(1)} all-to-all(bf16[32,2,2048]{2,1,0:T(2,128)(2,1)S(1)} %reshape.18), channel_id=1, replica_groups=mesh['gx'=32,'gz'=16] {'gx'}, dimensions={0} | all-to-all | bytes 524288 | tf_op jit(solution)/shard_map/all_to_all | solution.py:30
  69.8 0.4 reshape.19
  70.2 0.1 fusion.10
  70.2 0.3 copy.19
  70.6 0.2 reshape.17
  70.7 0.2 copy.20
  70.9 0.2 slice.20
  71.1 0.7 rev.3
  71.9 143.2 %all-gather.2.cloned.1.call-done = bf16[2,1024,1024]{2,1,0:T(8,128)(2,1)} async-done(((bf16[2,32,1024]{2,1,0:T(8,128)(2,1)}), bf16[2,1024,1024]{2,1,0:T(8,128)(2,1)}) %all-gather.2.cloned.1.call-update) | async-done | bytes 4194320 | tf_op jit(solution)/shard_map/all_gather | solution.py:39
  215.1 3.6 %fusion.2 = f32[2,1024,64]{1,2,0:T(8,128)S(1)} fusion(bf16[2,1024,1024]{2,1,0:T(8,128)(2,1)} %all-gather.2.cloned.1.call-done, bf16[1,1024,64]{1,2,0:T(8,128)(2,1)S(1)} %get-tuple-element.7, bf16[1,1024,64]{1,2,0:T(8,128)(2,1)S(1)} %get-tuple-element.6), kind=kOutput, calls=%fused_computation.5 | convolution fusion | flops 268566528 | bytes 4980736 | tf_op jit(solution)/shard_map/prj,pjc->prc/dot_general | solution.py:37
  218.7 0.6 copy.21
  219.2 1.1 reshape.20
  220.3 34.6 %all_to_all.32 = f32[32,1,4096]{2,1,0:T(1,128)S(1)} all-to-all(f32[32,1,4096]{2,1,0:T(1,128)S(1)} %reshape.20), channel_id=1, replica_groups=mesh['gx'=32,'gz'=16] {'gx'}, dimensions={0} | all-to-all | bytes 1048576 | tf_op jit(solution)/shard_map/all_to_all | solution.py:43
  255.0 0.5 broadcast
  255.5 1.9 reduce
  257.4 0.8 reshape.21
  258.1 0.1 copy.22
  258.2 0.1 fusion.9
  258.3 0.3 copy.23
  258.6 0.8 reshape_squeeze.6
  259.5 0.3 copy.24
  259.8 0.8 reshape_squeeze.7
  (2 shorter events, 0.1 us)
Async XLA Ops:
  7.2 207.9 %all-gather.2.cloned.1.call-start = ((), (), s32[]{:S(2)}) async-start(), calls=%async_computation.2 | async-start | bytes 4325376 | tf_op jit(solution)/shard_map/all_gather | solution.py:39
Sparse Core Ops, SparseCore 0:
  32.7 182.3 all-gather.1
where the time goes:
time: 268 us; the launch traced here: 267 us
  waiting for transfers between devices  143 us (53%)
  blocking collectives  92.8 us (35%)
  between operations  14.1 us (5%)
  local copies, waits for them, and re-layouts  10.9 us (4%)
  matrix products  3.57 us (1%)
  other arithmetic  2.75 us (1%)
    all_gather x1, waiting for transfers between devices, local(): lax.all_gather(stacked, 'gx', axis=1, tiled=True)  143 us
    all_to_all x1, blocking collectives, local(): lines = lax.all_to_all(flat, 'gx', split_axis=1, concat_axis=0, tiled=True)  35.5 us
    all_to_all x1, blocking collectives, local(): lax.all_to_all(all_modes, 'gx', split_axis=1, concat_axis=2, tiled=True)  34.6 us
    all_gather x1, blocking collectives, rows_first(): whole = lax.all_gather(both, axis, axis=0, tiled=True)  22.6 us
    unnamed x9, local copies, waits for them, and re-layouts  5.68 us
  transfers between devices with their start and end apart: 1, of which 1 were waited for; matrix products, arithmetic and copies ran while one was open for 1% of the time, Pallas kernels for 0%

commit v1 on v0

v1 whole, which is shorter than its diff:
```python
import jax
import jax.numpy as jnp
from jax import lax
from jax.experimental import pallas as pl
from jax.experimental.pallas import tpu as pltpu
from jax.sharding import PartitionSpec as P

MESH = pl.DeviceIdType.MESH
SIDE = 4
PLANE = 16
DEEP = 8
GROUP = 4
ROWS = 64
COLS = 128
MODES = 32
CHUNKS = 8
PER = PLANE // CHUNKS
HOPS = 8


def remote(src, dst, send, recv, target):
    return pltpu.make_async_remote_copy(
        src_ref=src, dst_ref=dst, send_sem=send, recv_sem=recv,
        device_id=target, device_id_type=MESH,
    )


def drain(ref, sem):
    pltpu.make_async_copy(ref, ref, sem).wait()


def kernel(field, even, odd, out_even, out_odd,
           wide, mine, own, far, relay, vecs, acc, sent, got,
           ring_recv, far_recv, recv, send):
    gx, gz = lax.axis_index("gx"), lax.axis_index("gz")
    half = gx // PLANE
    q = lax.rem(gx, PLANE)
    qy, qx = q // SIDE, lax.rem(q, SIDE)
    depth, core = gz // 2, lax.rem(gz, 2)
    z = half * DEEP + depth
    step = 1 - 2 * core

    def at(place, level):
        return ((level // DEEP) * PLANE + place, lax.rem(level, DEEP) * 2 + core)

    def level(k):
        return lax.rem(z + k * step + 2 * DEEP, 2 * DEEP)

    def place(t):
        return lax.rem(qy + t // SIDE, SIDE) * SIDE + lax.rem(qx + lax.rem(t, SIDE), SIDE)

    group = depth // GROUP
    ahead, behind = level(1), level(-1)
    across = half * DEEP + lax.rem(depth + GROUP, DEEP)
    mates = [half * DEEP + group * GROUP + lax.rem(depth + k, GROUP) for k in range(1, GROUP)]
    twin = (gx, gz + step)
    myrows = pl.ds(pl.multiple_of(q * MODES, MODES), MODES)

    barrier = pltpu.get_barrier_semaphore()

    def hello(target):
        pl.semaphore_signal(barrier, inc=1, device_id=target, device_id_type=MESH)

    for t in range(1, PLANE):
        hello(at(place(t), z))
    for t in range(PLANE):
        hello(at(place(t), behind))
    for m in mates:
        hello(at(q, m))
    hello(at(q, across))
    hello(twin)

    wide[...] = field[...].astype(jnp.float32)
    for p in range(PLANE):
        t = lax.rem(p // SIDE - qy + SIDE, SIDE) * SIDE + lax.rem(p % SIDE - qx + SIDE, SIDE)
        mine[t] = wide[pl.ds(p, ROWS, stride=PLANE), :].astype(jnp.bfloat16)
    own[q] = wide[pl.ds(q, ROWS, stride=PLANE), :].astype(jnp.bfloat16)
    vecs[depth, core, myrows, :] = jnp.concatenate([even[...], odd[...]], axis=1)

    pl.semaphore_wait(barrier, 2 * PLANE - 1 + GROUP + 1)

    for c in range(CHUNKS):
        remote(mine.at[pl.ds(c * PER, PER)], relay.at[c], send.at[0], ring_recv.at[c], at(q, ahead)).start()
    for m in mates:
        block = vecs.at[depth, core, myrows]
        remote(block, block, send.at[1], recv.at[0], at(q, m)).start()
    for t in range(1, PLANE):
        remote(mine.at[t], own.at[q], send.at[2], recv.at[1], at(place(t), z)).start()

    def spread(g, k):
        block = vecs.at[pl.ds(g * GROUP, GROUP), core, myrows]
        for t in range(1, PLANE):
            remote(block, block, send.at[3 + k], recv.at[2 + k], at(place(t), z)).start()

    def share(g, k):
        drain(vecs.at[pl.ds(0, GROUP), 0, pl.ds(0, (PLANE - 1) * MODES)], recv.at[2 + k])
        block = vecs.at[pl.ds(g * GROUP, GROUP), core]
        remote(block, block, send.at[5 + k], recv.at[4 + k], twin).start()

    def hop(first, last):
        @pl.loop(first * CHUNKS, last * CHUNKS)
        def _(i):
            drain(relay.at[i], ring_recv.at[i])
            remote(relay.at[i], relay.at[i + CHUNKS], send.at[7], ring_recv.at[i + CHUNKS], at(q, ahead)).start()

    drain(vecs.at[pl.ds(0, GROUP - 1), 0, pl.ds(0, MODES)], recv.at[0])
    block = vecs.at[pl.ds(group * GROUP, GROUP), core, myrows]
    remote(block, block, send.at[8], recv.at[6], at(q, across)).start()
    spread(group, 0)
    hop(0, 2)
    drain(vecs.at[pl.ds(0, GROUP), 0, pl.ds(0, MODES)], recv.at[6])
    spread(1 - group, 1)
    hop(2, 4)
    share(group, 0)
    hop(4, 6)
    share(1 - group, 1)

    @pl.loop(0, CHUNKS)
    def _(c):
        i = (HOPS - 2) * CHUNKS + c
        drain(relay.at[i], ring_recv.at[i])
        for h in range(PER):
            remote(relay.at[i, h], far.at[q], send.at[9], far_recv.at[qy], at(place(c * PER + h), ahead)).start()

    drain(own.at[pl.ds(0, PLANE - 1)], recv.at[1])
    drain(vecs.at[pl.ds(0, GROUP), 0], recv.at[4])
    drain(vecs.at[pl.ds(0, GROUP), 0], recv.at[5])
    wide_rows = SIDE * ROWS
    r = lax.broadcasted_iota(jnp.int32, (wide_rows, wide_rows), 0)
    s = lax.broadcasted_iota(jnp.int32, (wide_rows, wide_rows), 1)
    plain = (r == s).astype(jnp.float32).astype(jnp.bfloat16)
    turned = (r + s == wide_rows - 1).astype(jnp.float32).astype(jnp.bfloat16)
    zero = jnp.zeros((ROWS, COLS), jnp.bfloat16)

    def pick(first):
        return jnp.where(first, plain, turned)

    is_low = jnp.full((wide_rows, wide_rows), half, jnp.int32) == 0
    for_own = jnp.where(is_low, plain, turned)
    for_far = jnp.where(is_low, turned, plain)
    sign = (1 - 2 * half).astype(jnp.float32)
    for ty in range(SIDE):
        g = lax.rem(qy - ty + SIDE, SIDE)
        drain(far.at[pl.ds(0, SIDE)], far_recv.at[g])
        a = own[pl.ds((SIDE - 1 - g) * SIDE, SIDE)].reshape(wide_rows, COLS)
        b = far[pl.ds(g * SIDE, SIDE)].reshape(wide_rows, COLS)
        a = jnp.dot(for_own, a, preferred_element_type=jnp.float32)
        b = jnp.dot(for_far, b, preferred_element_type=jnp.float32)
        plus = (a + b).astype(jnp.bfloat16)
        minus = ((a - b) * sign).astype(jnp.bfloat16)
        j = jnp.where(half == 0, SIDE - 1 - g, g)
        left, right = [], []
        for k in range(2):
            for c in range(2):
                left.append(vecs[2 * j + k, c])
                rows = slice((2 * k + c) * ROWS, (2 * k + c + 1) * ROWS)
                right.append(jnp.concatenate([plus[rows], zero], axis=1))
                right.append(jnp.concatenate([zero, minus[rows]], axis=1))
        part = jnp.dot(jnp.concatenate(left, axis=1), jnp.concatenate(right, axis=0), preferred_element_type=jnp.float32)
        if ty == 0:
            acc[...] = part
        elif ty < SIDE - 1:
            acc[...] += part
        else:
            sent[...] = (acc[...] + part).astype(jnp.bfloat16).reshape(PLANE, MODES, 2 * COLS)

    for t in range(1, PLANE):
        remote(sent.at[place(t)], got.at[q], send.at[10], recv.at[7], at(place(t), z)).start()
    got[q] = sent[q]
    drain(got.at[pl.ds(0, PLANE - 1)], recv.at[7])
    for p in range(PLANE):
        block = got[p].astype(jnp.float32)
        out_even[pl.ds(p, MODES, stride=PLANE), :] = block[:, :COLS]
        out_odd[pl.ds(p, MODES, stride=PLANE), :] = block[:, COLS:]

    drain(mine, send.at[0])
    drain(vecs.at[pl.ds(0, GROUP - 1), 0, pl.ds(0, MODES)], send.at[1])
    drain(mine.at[pl.ds(0, PLANE - 1)], send.at[2])
    for k in range(2):
        drain(vecs.at[pl.ds(0, GROUP), 0, pl.ds(0, (PLANE - 1) * MODES)], send.at[3 + k])
        drain(vecs.at[pl.ds(0, GROUP), 0], send.at[5 + k])
    drain(relay.at[pl.ds(0, (HOPS - 2) * CHUNKS)], send.at[7])
    drain(vecs.at[pl.ds(0, GROUP), 0, pl.ds(0, MODES)], send.at[8])
    drain(mine, send.at[9])
    drain(got.at[pl.ds(0, PLANE - 1)], send.at[10])


def local(field, even_vectors, odd_vectors):
    out = jax.ShapeDtypeStruct((MODES * PLANE, COLS), jnp.float32)
    vmem = pl.BlockSpec(memory_space=pltpu.VMEM)
    slots = (HOPS - 1) * CHUNKS
    even_modes, odd_modes = pl.pallas_call(
        kernel,
        out_shape=(out, out),
        in_specs=[vmem] * 3,
        out_specs=(vmem, vmem),
        scratch_shapes=[
            pltpu.VMEM((ROWS * PLANE, COLS), jnp.float32),
            pltpu.VMEM((PLANE, ROWS, COLS), jnp.bfloat16),
            pltpu.VMEM((PLANE, ROWS, COLS), jnp.bfloat16),
            pltpu.VMEM((PLANE, ROWS, COLS), jnp.bfloat16),
            pltpu.VMEM((slots, PER, ROWS, COLS), jnp.bfloat16),
            pltpu.VMEM((DEEP, 2, PLANE * MODES, COLS), jnp.bfloat16),
            pltpu.VMEM((PLANE * MODES, 2 * COLS), jnp.float32),
            pltpu.VMEM((PLANE, MODES, 2 * COLS), jnp.bfloat16),
            pltpu.VMEM((PLANE, MODES, 2 * COLS), jnp.bfloat16),
            pltpu.SemaphoreType.DMA((slots,)),
            pltpu.SemaphoreType.DMA((SIDE,)),
            pltpu.SemaphoreType.DMA((8,)),
            pltpu.SemaphoreType.DMA((11,)),
        ],
        compiler_params=pltpu.CompilerParams(collective_id=0, has_side_effects=True),
    )(field.reshape(ROWS * PLANE, COLS), even_vectors, odd_vectors)
    return even_modes.reshape(MODES, PLANE, COLS), odd_modes.reshape(MODES, PLANE, COLS)


def solution(mesh):
    return jax.shard_map(
        local,
        mesh=mesh,
        in_specs=(P("gx", None, "gz"), P("gx", "gz"), P("gx", "gz")),
        out_specs=(P("gx", None, "gz"), P("gx", None, "gz")),
        check_vma=False,
    )
```

time: 268 us -> 60.3 us (0.22)
  the two profiles are of different devices: /device:TPU:96 before, /device:TPU:32 now
where the time goes in v1:
time: 60.3 us; the launch traced here: 60.2 us
  Pallas kernels  57.1 us (95%)
  local copies, waits for them, and re-layouts  2.42 us (4%)
  between operations  0.65 us (1%)
    pallas_call x1, Pallas kernels, local(): pl.pallas_call(kernel, out_shape=(out, out), in_specs=[vmem] * 3, out_spe...  57.1 us
    unnamed x4, local copies, waits for them, and re-layouts  2.42 us

profile of v1, /device:TPU:32, one launch (start us, length us, event | category | flops | bytes accessed | tf_op | source)
XLA Modules:
  0.0 60.2 jit_solution(1304737957922244341)
XLA Ops:
  0.6 57.1 %shard_map.50 = (f32[512,128]{1,0:T(8,128)}, f32[512,128]{1,0:T(8,128)}) custom-call(bf16[1024,128]{1,0:T(8,128)(2,1)} %bitcast.3, bf16[32,64]{1,0:T(8,128)(2,1)} %even.1, bf16[32,64]{1,0:T(8,128)(2,1)} %odd.1), custom_call_target="tpu_custom_call" | custom-call | tf_op jit(solution)/shard_map/pallas_call | solution.py:192
  57.7 0.0 copy-start
  57.8 1.7 %copy.7 = f32[32,16,128]{2,1,0:T(8,128)} copy(f32[32,16,128]{2,1,0:T(8,128)} %bitcast.5) | data formatting | bytes 524288
  59.5 0.0 copy-done
  59.5 0.7 %copy.8 = f32[32,16,128]{2,1,0:T(8,128)} copy(f32[32,16,128]{2,1,0:T(8,128)S(1)} %bitcast.4) | data formatting | bytes 524288
Async XLA Ops:
  57.7 1.7 %copy-start = (f32[512,128]{1,0:T(8,128)S(1)}, f32[512,128]{1,0:T(8,128)}, u32[]{:S(2)}) copy-start(f32[512,128]{1,0:T(8,128)} %get-tuple-element.5) | copy-start | bytes 786436

commit v2 on v1

--- a/solution.py
+++ b/solution.py
@@ -16,6 +16,7 @@
 CHUNKS = 8
 PER = PLANE // CHUNKS
 HOPS = 8
+FAR_FIRST = (2, 3, 1, 0)
 
 
 def remote(src, dst, send, recv, target):
@@ -29,9 +30,11 @@
     pltpu.make_async_copy(ref, ref, sem).wait()
 
 
-def kernel(field, even, odd, out_even, out_odd,
-           wide, mine, own, far, relay, vecs, acc, sent, got,
+def kernel(field, even, odd, out,
+           raw, wide, mine, own, far, relay, vecs, acc, sent, got,
            ring_recv, far_recv, recv, send):
+    fetch = pltpu.make_async_copy(field, raw, send.at[11])
+    fetch.start()
     gx, gz = lax.axis_index("gx"), lax.axis_index("gz")
     half = gx // PLANE
     q = lax.rem(gx, PLANE)
@@ -46,8 +49,13 @@
     def level(k):
         return lax.rem(z + k * step + 2 * DEEP, 2 * DEEP)
 
+    def offset(i):
+        if isinstance(i, int):
+            return FAR_FIRST[i]
+        return (1 - i // 2) * (2 + i) + (i // 2) * (3 - i)
+
     def place(t):
-        return lax.rem(qy + t // SIDE, SIDE) * SIDE + lax.rem(qx + lax.rem(t, SIDE), SIDE)
+        return lax.rem(qy + offset(t // SIDE), SIDE) * SIDE + lax.rem(qx + offset(t % SIDE if isinstance(t, int) else lax.rem(t, SIDE)), SIDE)
 
     group = depth // GROUP
     ahead, behind = level(1), level(-1)
@@ -61,7 +69,7 @@
     def hello(target):
         pl.semaphore_signal(barrier, inc=1, device_id=target, device_id_type=MESH)
 
-    for t in range(1, PLANE):
+    for t in range(PLANE - 1):
         hello(at(place(t), z))
     for t in range(PLANE):
         hello(at(place(t), behind))
@@ -70,26 +78,26 @@
     hello(at(q, across))
     hello(twin)
 
-    wide[...] = field[...].astype(jnp.float32)
-    for p in range(PLANE):
-        t = lax.rem(p // SIDE - qy + SIDE, SIDE) * SIDE + lax.rem(p % SIDE - qx + SIDE, SIDE)
-        mine[t] = wide[pl.ds(p, ROWS, stride=PLANE), :].astype(jnp.bfloat16)
-    own[q] = wide[pl.ds(q, ROWS, stride=PLANE), :].astype(jnp.bfloat16)
+    fetch.wait()
+    wide[...] = raw[...].astype(jnp.float32)
+    for t in range(PLANE):
+        mine[t] = wide[pl.ds(place(t), ROWS, stride=PLANE), :].astype(jnp.bfloat16)
+    own[q] = mine[PLANE - 1]
     vecs[depth, core, myrows, :] = jnp.concatenate([even[...], odd[...]], axis=1)
 
     pl.semaphore_wait(barrier, 2 * PLANE - 1 + GROUP + 1)
 
-    for c in range(CHUNKS):
-        remote(mine.at[pl.ds(c * PER, PER)], relay.at[c], send.at[0], ring_recv.at[c], at(q, ahead)).start()
     for m in mates:
         block = vecs.at[depth, core, myrows]
         remote(block, block, send.at[1], recv.at[0], at(q, m)).start()
-    for t in range(1, PLANE):
+    for c in range(CHUNKS):
+        remote(mine.at[pl.ds(c * PER, PER)], relay.at[c], send.at[0], ring_recv.at[c], at(q, ahead)).start()
+    for t in range(PLANE - 1):
         remote(mine.at[t], own.at[q], send.at[2], recv.at[1], at(place(t), z)).start()
 
     def spread(g, k):
         block = vecs.at[pl.ds(g * GROUP, GROUP), core, myrows]
-        for t in range(1, PLANE):
+        for t in range(PLANE - 1):
             remote(block, block, send.at[3 + k], recv.at[2 + k], at(place(t), z)).start()
 
     def share(g, k):
@@ -103,16 +111,17 @@
             drain(relay.at[i], ring_recv.at[i])
             remote(relay.at[i], relay.at[i + CHUNKS], send.at[7], ring_recv.at[i + CHUNKS], at(q, ahead)).start()
 
+    hop(0, 1)
     drain(vecs.at[pl.ds(0, GROUP - 1), 0, pl.ds(0, MODES)], recv.at[0])
     block = vecs.at[pl.ds(group * GROUP, GROUP), core, myrows]
     remote(block, block, send.at[8], recv.at[6], at(q, across)).start()
     spread(group, 0)
-    hop(0, 2)
+    hop(1, 3)
     drain(vecs.at[pl.ds(0, GROUP), 0, pl.ds(0, MODES)], recv.at[6])
     spread(1 - group, 1)
-    hop(2, 4)
+    hop(3, 5)
     share(group, 0)
-    hop(4, 6)
+    hop(5, 6)
     share(1 - group, 1)
 
     @pl.loop(0, CHUNKS)
@@ -140,7 +149,7 @@
     for_far = jnp.where(is_low, turned, plain)
     sign = (1 - 2 * half).astype(jnp.float32)
     for ty in range(SIDE):
-        g = lax.rem(qy - ty + SIDE, SIDE)
+        g = lax.rem(qy - offset(ty) + SIDE, SIDE)
         drain(far.at[pl.ds(0, SIDE)], far_recv.at[g])
         a = own[pl.ds((SIDE - 1 - g) * SIDE, SIDE)].reshape(wide_rows, COLS)
         b = far[pl.ds(g * SIDE, SIDE)].reshape(wide_rows, COLS)
@@ -164,14 +173,11 @@
         else:
             sent[...] = (acc[...] + part).astype(jnp.bfloat16).reshape(PLANE, MODES, 2 * COLS)
 
-    for t in range(1, PLANE):
+    for t in range(PLANE - 1):
         remote(sent.at[place(t)], got.at[q], send.at[10], recv.at[7], at(place(t), z)).start()
     got[q] = sent[q]
     drain(got.at[pl.ds(0, PLANE - 1)], recv.at[7])
-    for p in range(PLANE):
-        block = got[p].astype(jnp.float32)
-        out_even[pl.ds(p, MODES, stride=PLANE), :] = block[:, :COLS]
-        out_odd[pl.ds(p, MODES, stride=PLANE), :] = block[:, COLS:]
+    out[...] = got[...]
 
     drain(mine, send.at[0])
     drain(vecs.at[pl.ds(0, GROUP - 1), 0, pl.ds(0, MODES)], send.at[1])
@@ -185,16 +191,24 @@
     drain(got.at[pl.ds(0, PLANE - 1)], send.at[10])
 
 
+def unpack(got, out_even, out_odd):
+    rows = got.shape[1]
+    for p in range(PLANE):
+        block = got[p].astype(jnp.float32)
+        out_even[pl.ds(p, rows, stride=PLANE), :] = block[:, :COLS]
+        out_odd[pl.ds(p, rows, stride=PLANE), :] = block[:, COLS:]
+
+
 def local(field, even_vectors, odd_vectors):
-    out = jax.ShapeDtypeStruct((MODES * PLANE, COLS), jnp.float32)
     vmem = pl.BlockSpec(memory_space=pltpu.VMEM)
     slots = (HOPS - 1) * CHUNKS
-    even_modes, odd_modes = pl.pallas_call(
+    modes = pl.pallas_call(
         kernel,
-        out_shape=(out, out),
-        in_specs=[vmem] * 3,
-        out_specs=(vmem, vmem),
+        out_shape=jax.ShapeDtypeStruct((PLANE, MODES, 2 * COLS), jnp.bfloat16),
+        in_specs=[pl.BlockSpec(memory_space=pl.ANY), vmem, vmem],
+        out_specs=vmem,
         scratch_shapes=[
+            pltpu.VMEM((ROWS * PLANE, COLS), jnp.bfloat16),
             pltpu.VMEM((ROWS * PLANE, COLS), jnp.float32),
             pltpu.VMEM((PLANE, ROWS, COLS), jnp.bfloat16),
             pltpu.VMEM((PLANE, ROWS, COLS), jnp.bfloat16),
@@ -207,10 +221,20 @@
             pltpu.SemaphoreType.DMA((slots,)),
             pltpu.SemaphoreType.DMA((SIDE,)),
             pltpu.SemaphoreType.DMA((8,)),
-            pltpu.SemaphoreType.DMA((11,)),
+            pltpu.SemaphoreType.DMA((12,)),
         ],
         compiler_params=pltpu.CompilerParams(collective_id=0, has_side_effects=True),
     )(field.reshape(ROWS * PLANE, COLS), even_vectors, odd_vectors)
+    parts = 2
+    rows = MODES // parts
+    out = jax.ShapeDtypeStruct((MODES * PLANE, COLS), jnp.float32)
+    even_modes, odd_modes = pl.pallas_call(
+        unpack,
+        grid=(parts,),
+        out_shape=(out, out),
+        in_specs=[pl.BlockSpec((PLANE, rows, 2 * COLS), lambda i: (0, i, 0))],
+        out_specs=[pl.BlockSpec((rows * PLANE, COLS), lambda i: (i, 0))] * 2,
+    )(modes)
     return even_modes.reshape(MODES, PLANE, COLS), odd_modes.reshape(MODES, PLANE, COLS)
 
 

time: 60.3 us -> 56.6 us (0.939)
  local copies, waits for them, and re-layouts: 2.42 us -> 0 us
  Pallas kernels: 57.1 us -> 55.8 us
    unnamed x4 -> x0, local copies, waits for them, and re-layouts: 2.42 us -> none
    pallas_call x1 -> x2, Pallas kernels: 57.1 us -> 55.8 us  [the longest x1 53.9 us: local(): pl.pallas_call(kernel, out_shape=jax.ShapeDtypeStruct((PLANE, MODES, 2 *...]
where the time goes in v2:
time: 56.6 us; the launch traced here: 56.4 us
  Pallas kernels  55.8 us (99%)
  between operations  0.64 us (1%)
    pallas_call x1, Pallas kernels, local(): pl.pallas_call(kernel, out_shape=jax.ShapeDtypeStruct((PLANE, MODES, 2 *...  53.9 us
    pallas_call x1, Pallas kernels, local(): pl.pallas_call(unpack, grid=(parts,), out_shape=(out, out), in_specs=[pl....  1.85 us

profile of v2, /device:TPU:32, one launch (start us, length us, event | category | flops | bytes accessed | tf_op | source)
XLA Modules:
  0.0 56.4 jit_solution(10357939444539413537)
XLA Ops:
  0.6 53.9 %shard_map.50.got = bf16[16,32,256]{2,1,0:T(8,128)(2,1)} custom-call(bf16[1024,128]{1,0:T(8,128)(2,1)} %bitcast.3, bf16[32,64]{1,0:T(8,128)(2,1)} %even.1, bf16[32,64]{1,0:T(8,128)(2,1)} %odd.1), custom_call_target="tpu_custom_call" | custom-call | tf_op jit(solution)/shard_map/pallas_call | solution.py:205
  54.6 1.8 %shard_map.51 = (f32[512,128]{1,0:T(8,128)}, f32[512,128]{1,0:T(8,128)}) custom-call(bf16[16,32,256]{2,1,0:T(8,128)(2,1)} %shard_map.50.got), custom_call_target="tpu_custom_call" | custom-call | tf_op jit(solution)/shard_map/pallas_call | solution.py:231

commit v3 on v2

--- a/solution.py
+++ b/solution.py
@@ -30,18 +30,23 @@
     pltpu.make_async_copy(ref, ref, sem).wait()
 
 
-def kernel(field, even, odd, out,
-           raw, wide, mine, own, far, relay, vecs, acc, sent, got,
-           ring_recv, far_recv, recv, send):
-    fetch = pltpu.make_async_copy(field, raw, send.at[11])
-    fetch.start()
+def kernel(field, even_hbm, odd_hbm, out,
+           raw, even, odd, wide, mine, own, far, relay, vecs, acc, sent, got,
+           ring_recv, far_recv, recv, send, ready):
+    fetches = [
+        pltpu.make_async_copy(field, raw, send.at[9]),
+        pltpu.make_async_copy(even_hbm, even, send.at[11]),
+        pltpu.make_async_copy(odd_hbm, odd, send.at[12]),
+    ]
+    for fetch in fetches:
+        fetch.start()
     gx, gz = lax.axis_index("gx"), lax.axis_index("gz")
     half = gx // PLANE
     q = lax.rem(gx, PLANE)
     qy, qx = q // SIDE, lax.rem(q, SIDE)
     depth, core = gz // 2, lax.rem(gz, 2)
     z = half * DEEP + depth
-    step = 1 - 2 * core
+    step = 2 * core - 1
 
     def at(place, level):
         return ((level // DEEP) * PLANE + place, lax.rem(level, DEEP) * 2 + core)
@@ -61,7 +66,7 @@
     ahead, behind = level(1), level(-1)
     across = half * DEEP + lax.rem(depth + GROUP, DEEP)
     mates = [half * DEEP + group * GROUP + lax.rem(depth + k, GROUP) for k in range(1, GROUP)]
-    twin = (gx, gz + step)
+    twin = (gx, gz + 1 - 2 * core)
     myrows = pl.ds(pl.multiple_of(q * MODES, MODES), MODES)
 
     barrier = pltpu.get_barrier_semaphore()
@@ -71,27 +76,29 @@
 
     for t in range(PLANE - 1):
         hello(at(place(t), z))
-    for t in range(PLANE):
-        hello(at(place(t), behind))
+    hello(at(q, ahead))
+    hello(at(q, behind))
     for m in mates:
         hello(at(q, m))
     hello(at(q, across))
     hello(twin)
 
-    fetch.wait()
+    for fetch in fetches:
+        fetch.wait()
     wide[...] = raw[...].astype(jnp.float32)
     for t in range(PLANE):
         mine[t] = wide[pl.ds(place(t), ROWS, stride=PLANE), :].astype(jnp.bfloat16)
     own[q] = mine[PLANE - 1]
     vecs[depth, core, myrows, :] = jnp.concatenate([even[...], odd[...]], axis=1)
 
-    pl.semaphore_wait(barrier, 2 * PLANE - 1 + GROUP + 1)
+    pl.semaphore_wait(barrier, PLANE - 1 + 2 + GROUP + 1)
 
     for m in mates:
         block = vecs.at[depth, core, myrows]
         remote(block, block, send.at[1], recv.at[0], at(q, m)).start()
     for c in range(CHUNKS):
         remote(mine.at[pl.ds(c * PER, PER)], relay.at[c], send.at[0], ring_recv.at[c], at(q, ahead)).start()
+    pl.semaphore_signal(ready, inc=1, device_id=at(q, behind), device_id_type=MESH)
     for t in range(PLANE - 1):
         remote(mine.at[t], own.at[q], send.at[2], recv.at[1], at(place(t), z)).start()
 
@@ -124,12 +131,14 @@
     hop(5, 6)
     share(1 - group, 1)
 
+    pl.semaphore_wait(ready, 1)
+
     @pl.loop(0, CHUNKS)
     def _(c):
         i = (HOPS - 2) * CHUNKS + c
         drain(relay.at[i], ring_recv.at[i])
         for h in range(PER):
-            remote(relay.at[i, h], far.at[q], send.at[9], far_recv.at[qy], at(place(c * PER + h), ahead)).start()
+            remote(relay.at[i, h], far.at[q], send.at[13], far_recv.at[qy], at(place(c * PER + h), ahead)).start()
 
     drain(own.at[pl.ds(0, PLANE - 1)], recv.at[1])
     drain(vecs.at[pl.ds(0, GROUP), 0], recv.at[4])
@@ -187,7 +196,7 @@
         drain(vecs.at[pl.ds(0, GROUP), 0], send.at[5 + k])
     drain(relay.at[pl.ds(0, (HOPS - 2) * CHUNKS)], send.at[7])
     drain(vecs.at[pl.ds(0, GROUP), 0, pl.ds(0, MODES)], send.at[8])
-    drain(mine, send.at[9])
+    drain(mine, send.at[13])
     drain(got.at[pl.ds(0, PLANE - 1)], send.at[10])
 
 
@@ -205,10 +214,12 @@
     modes = pl.pallas_call(
         kernel,
         out_shape=jax.ShapeDtypeStruct((PLANE, MODES, 2 * COLS), jnp.bfloat16),
-        in_specs=[pl.BlockSpec(memory_space=pl.ANY), vmem, vmem],
+        in_specs=[pl.BlockSpec(memory_space=pltpu.HBM)] * 3,
         out_specs=vmem,
         scratch_shapes=[
             pltpu.VMEM((ROWS * PLANE, COLS), jnp.bfloat16),
+            pltpu.VMEM((MODES, ROWS), jnp.bfloat16),
+            pltpu.VMEM((MODES, ROWS), jnp.bfloat16),
             pltpu.VMEM((ROWS * PLANE, COLS), jnp.float32),
             pltpu.VMEM((PLANE, ROWS, COLS), jnp.bfloat16),
             pltpu.VMEM((PLANE, ROWS, COLS), jnp.bfloat16),
@@ -221,9 +232,10 @@
             pltpu.SemaphoreType.DMA((slots,)),
             pltpu.SemaphoreType.DMA((SIDE,)),
             pltpu.SemaphoreType.DMA((8,)),
-            pltpu.SemaphoreType.DMA((12,)),
+            pltpu.SemaphoreType.DMA((14,)),
+            pltpu.SemaphoreType.REGULAR,
         ],
-        compiler_params=pltpu.CompilerParams(collective_id=0, has_side_effects=True),
+        compiler_params=pltpu.CompilerParams(collective_id=0, has_side_effects=True, vmem_limit_bytes=16 * 1024 * 1024),
     )(field.reshape(ROWS * PLANE, COLS), even_vectors, odd_vectors)
     parts = 2
     rows = MODES // parts
@@ -234,6 +246,7 @@
         out_shape=(out, out),
         in_specs=[pl.BlockSpec((PLANE, rows, 2 * COLS), lambda i: (0, i, 0))],
         out_specs=[pl.BlockSpec((rows * PLANE, COLS), lambda i: (i, 0))] * 2,
+        compiler_params=pltpu.CompilerParams(vmem_limit_bytes=8 * 1024 * 1024),
     )(modes)
     return even_modes.reshape(MODES, PLANE, COLS), odd_modes.reshape(MODES, PLANE, COLS)
 

time: 56.6 us -> 53.7 us (0.949)
  the two profiles are of different devices: /device:TPU:32 before, /device:TPU:1 now
where the time goes in v3:
time: 53.7 us; the launch traced here: 53.4 us
  Pallas kernels  50.4 us (94%)
  local copies, waits for them, and re-layouts  2.34 us (4%)
  between operations  0.65 us (1%)
    pallas_call x1, Pallas kernels, local(): pl.pallas_call(kernel, out_shape=jax.ShapeDtypeStruct((PLANE, MODES, 2 *...  49.5 us
    unnamed x6, local copies, waits for them, and re-layouts  2.34 us

profile of v3, /device:TPU:1, one launch (start us, length us, event | category | flops | bytes accessed | tf_op | source)
XLA Modules:
  0.0 53.4 jit_solution(10010458727892318029)
XLA Ops:
  0.6 0.0 copy-start
  0.6 0.9 %copy-done = bf16[64,16,128]{2,1,0:T(8,128)(2,1)S(1)} copy-done((bf16[64,16,128]{2,1,0:T(8,128)(2,1)S(1)}, bf16[64,16,128]{2,1,0:T(8,128)(2,1)}, u32[]{:S(2)}) %copy-start) | copy-done | bytes 262168
  1.6 0.0 copy-start.1
  1.6 0.7 %copy-done.1 = bf16[32,64]{1,0:T(8,128)(2,1)S(1)} copy-done((bf16[32,64]{1,0:T(8,128)(2,1)S(1)}, bf16[32,64]{1,0:T(8,128)(2,1)}, u32[]{:S(2)}) %copy-start.1) | copy-done | bytes 4120
  2.3 0.0 copy-start.2
  2.3 0.7 %copy-done.2 = bf16[32,64]{1,0:T(8,128)(2,1)S(1)} copy-done((bf16[32,64]{1,0:T(8,128)(2,1)S(1)}, bf16[32,64]{1,0:T(8,128)(2,1)}, u32[]{:S(2)}) %copy-start.2) | copy-done | bytes 4120
  3.0 49.5 %shard_map.50.got = bf16[16,32,256]{2,1,0:T(8,128)(2,1)S(1)} custom-call(bf16[1024,128]{1,0:T(8,128)(2,1)S(1)} %bitcast.3, bf16[32,64]{1,0:T(8,128)(2,1)S(1)} %copy-done.1, bf16[32,64]{1,0:T(8,128)(2,1)S(1)} %copy-done.2), custom_call_target="tpu_custom_call" | custom-call | tf_op jit(solution)/shard_map/pallas_call | solution.py:214
  52.4 1.0 %shard_map.51 = (f32[512,128]{1,0:T(8,128)}, f32[512,128]{1,0:T(8,128)}) custom-call(bf16[16,32,256]{2,1,0:T(8,128)(2,1)S(1)} %shard_map.50.got), custom_call_target="tpu_custom_call" | custom-call | tf_op jit(solution)/shard_map/pallas_call | solution.py:243
Async XLA Ops:
  0.6 1.0 %copy-start = (bf16[64,16,128]{2,1,0:T(8,128)(2,1)S(1)}, bf16[64,16,128]{2,1,0:T(8,128)(2,1)}, u32[]{:S(2)}) copy-start(bf16[64,16,128]{2,1,0:T(8,128)(2,1)} %param.3) | copy-start | bytes 786436
  1.6 0.7 %copy-start.1 = (bf16[32,64]{1,0:T(8,128)(2,1)S(1)}, bf16[32,64]{1,0:T(8,128)(2,1)}, u32[]{:S(2)}) copy-start(bf16[32,64]{1,0:T(8,128)(2,1)} %even_hbm.1) | copy-start | bytes 12292
  2.3 0.7 %copy-start.2 = (bf16[32,64]{1,0:T(8,128)(2,1)S(1)}, bf16[32,64]{1,0:T(8,128)(2,1)}, u32[]{:S(2)}) copy-start(bf16[32,64]{1,0:T(8,128)(2,1)} %odd_hbm.1) | copy-start | bytes 12292

commit v4 on v3

--- a/solution.py
+++ b/solution.py
@@ -236,7 +236,7 @@
             pltpu.SemaphoreType.REGULAR,
         ],
         compiler_params=pltpu.CompilerParams(collective_id=0, has_side_effects=True, vmem_limit_bytes=16 * 1024 * 1024),
-    )(field.reshape(ROWS * PLANE, COLS), even_vectors, odd_vectors)
+    )(*(pltpu.with_memory_space_constraint(v, pltpu.HBM) for v in (field.reshape(ROWS * PLANE, COLS), even_vectors, odd_vectors)))
     parts = 2
     rows = MODES // parts
     out = jax.ShapeDtypeStruct((MODES * PLANE, COLS), jnp.float32)

time: 53.7 us -> 51.2 us (0.953)
  local copies, waits for them, and re-layouts: 2.34 us -> 0 us
    unnamed x6 -> x0, local copies, waits for them, and re-layouts: 2.34 us -> none
where the time goes in v4:
time: 51.2 us; the launch traced here: 51 us
  Pallas kernels  50.4 us (98%)
  between operations  0.64 us (1%)
    pallas_call x1, Pallas kernels, local(): pl.pallas_call(kernel, out_shape=jax.ShapeDtypeStruct((PLANE, MODES, 2 *...  49.4 us

profile of v4, /device:TPU:1, one launch (start us, length us, event | category | flops | bytes accessed | tf_op | source)
XLA Modules:
  0.0 51.0 jit_solution(14079823962662513122)
XLA Ops:
  0.6 49.4 %shard_map.50.got = bf16[16,32,256]{2,1,0:T(8,128)(2,1)S(1)} custom-call(bf16[1024,128]{1,0:T(8,128)(2,1)} %bitcast.3, bf16[32,64]{1,0:T(8,128)(2,1)} %even_hbm.1, bf16[32,64]{1,0:T(8,128)(2,1)} %odd_hbm.1), custom_call_target="tpu_custom_call" | custom-call | tf_op jit(solution)/shard_map/pallas_call | solution.py:214
  50.1 1.0 %shard_map.51 = (f32[512,128]{1,0:T(8,128)}, f32[512,128]{1,0:T(8,128)}) custom-call(bf16[16,32,256]{2,1,0:T(8,128)(2,1)S(1)} %shard_map.50.got), custom_call_target="tpu_custom_call" | custom-call | tf_op jit(solution)/shard_map/pallas_call | solution.py:243

commit v5 on v4

--- a/solution.py
+++ b/solution.py
@@ -13,7 +13,7 @@
 ROWS = 64
 COLS = 128
 MODES = 32
-CHUNKS = 8
+CHUNKS = 16
 PER = PLANE // CHUNKS
 HOPS = 8
 FAR_FIRST = (2, 3, 1, 0)
@@ -74,13 +74,13 @@
     def hello(target):
         pl.semaphore_signal(barrier, inc=1, device_id=target, device_id_type=MESH)
 
+    hello(at(q, across))
+    for m in mates:
+        hello(at(q, m))
+    hello(at(q, ahead))
+    hello(at(q, behind))
     for t in range(PLANE - 1):
         hello(at(place(t), z))
-    hello(at(q, ahead))
-    hello(at(q, behind))
-    for m in mates:
-        hello(at(q, m))
-    hello(at(q, across))
     hello(twin)
 
     for fetch in fetches:
@@ -159,10 +159,10 @@
     sign = (1 - 2 * half).astype(jnp.float32)
     for ty in range(SIDE):
         g = lax.rem(qy - offset(ty) + SIDE, SIDE)
+        a = own[pl.ds((SIDE - 1 - g) * SIDE, SIDE)].reshape(wide_rows, COLS)
+        a = jnp.dot(for_own, a, preferred_element_type=jnp.float32)
         drain(far.at[pl.ds(0, SIDE)], far_recv.at[g])
-        a = own[pl.ds((SIDE - 1 - g) * SIDE, SIDE)].reshape(wide_rows, COLS)
         b = far[pl.ds(g * SIDE, SIDE)].reshape(wide_rows, COLS)
-        a = jnp.dot(for_own, a, preferred_element_type=jnp.float32)
         b = jnp.dot(for_far, b, preferred_element_type=jnp.float32)
         plus = (a + b).astype(jnp.bfloat16)
         minus = ((a - b) * sign).astype(jnp.bfloat16)

time: 51.2 us -> 51.1 us (level)
  no operation moved by 1% of the time
where the time goes in v5:
time: 51.1 us; the launch traced here: 51 us
  Pallas kernels  50.3 us (98%)
  between operations  0.64 us (1%)
    pallas_call x1, Pallas kernels, local(): pl.pallas_call(kernel, out_shape=jax.ShapeDtypeStruct((PLANE, MODES, 2 *...  49.4 us

profile of v5, /device:TPU:1, one launch (start us, length us, event | category | flops | bytes accessed | tf_op | source)
XLA Modules:
  0.0 51.0 jit_solution(12151571539981099357)
XLA Ops:
  0.6 49.4 %shard_map.50.got = bf16[16,32,256]{2,1,0:T(8,128)(2,1)S(1)} custom-call(bf16[1024,128]{1,0:T(8,128)(2,1)} %bitcast.3, bf16[32,64]{1,0:T(8,128)(2,1)} %even_hbm.1, bf16[32,64]{1,0:T(8,128)(2,1)} %odd_hbm.1), custom_call_target="tpu_custom_call" | custom-call | tf_op jit(solution)/shard_map/pallas_call | solution.py:214
  50.0 1.0 %shard_map.51 = (f32[512,128]{1,0:T(8,128)}, f32[512,128]{1,0:T(8,128)}) custom-call(bf16[16,32,256]{2,1,0:T(8,128)(2,1)S(1)} %shard_map.50.got), custom_call_target="tpu_custom_call" | custom-call | tf_op jit(solution)/shard_map/pallas_call | solution.py:243

commit v6 on v5

--- a/solution.py
+++ b/solution.py
@@ -185,9 +185,6 @@
     for t in range(PLANE - 1):
         remote(sent.at[place(t)], got.at[q], send.at[10], recv.at[7], at(place(t), z)).start()
     got[q] = sent[q]
-    drain(got.at[pl.ds(0, PLANE - 1)], recv.at[7])
-    out[...] = got[...]
-
     drain(mine, send.at[0])
     drain(vecs.at[pl.ds(0, GROUP - 1), 0, pl.ds(0, MODES)], send.at[1])
     drain(mine.at[pl.ds(0, PLANE - 1)], send.at[2])
@@ -197,6 +194,9 @@
     drain(relay.at[pl.ds(0, (HOPS - 2) * CHUNKS)], send.at[7])
     drain(vecs.at[pl.ds(0, GROUP), 0, pl.ds(0, MODES)], send.at[8])
     drain(mine, send.at[13])
+    drain(got.at[pl.ds(0, PLANE - 1)], recv.at[7])
+    out[...] = got[...]
+
     drain(got.at[pl.ds(0, PLANE - 1)], send.at[10])
 
 

time: 51.1 us -> 51.1 us (level)
  no operation moved by 1% of the time
where the time goes in v6:
time: 51.1 us; the launch traced here: 51 us
  Pallas kernels  50.3 us (98%)
  between operations  0.64 us (1%)
    pallas_call x1, Pallas kernels, local(): pl.pallas_call(kernel, out_shape=jax.ShapeDtypeStruct((PLANE, MODES, 2 *...  49.3 us

profile of v6, /device:TPU:1, one launch (start us, length us, event | category | flops | bytes accessed | tf_op | source)
XLA Modules:
  0.0 51.0 jit_solution(3306261382811901183)
XLA Ops:
  0.6 49.3 %shard_map.50.got = bf16[16,32,256]{2,1,0:T(8,128)(2,1)S(1)} custom-call(bf16[1024,128]{1,0:T(8,128)(2,1)} %bitcast.3, bf16[32,64]{1,0:T(8,128)(2,1)} %even_hbm.1, bf16[32,64]{1,0:T(8,128)(2,1)} %odd_hbm.1), custom_call_target="tpu_custom_call" | custom-call | tf_op jit(solution)/shard_map/pallas_call | solution.py:214
  50.0 1.0 %shard_map.51 = (f32[512,128]{1,0:T(8,128)}, f32[512,128]{1,0:T(8,128)}) custom-call(bf16[16,32,256]{2,1,0:T(8,128)(2,1)S(1)} %shard_map.50.got), custom_call_target="tpu_custom_call" | custom-call | tf_op jit(solution)/shard_map/pallas_call | solution.py:243
